TPU v7x, 256 devices: a whole 4x4x8 slice. The times are simulated.
256 devices in a mesh: section: 8 (over x, z_hi), expert: 8 (over z_lo, core), tensor: 4 (over y).
Axes of the slice: x: 4, y: 4, z: 8 (z_hi: 2, z_lo: 4; z = z_hi * 4 + z_lo), core: 2. Of those that a mesh axis runs over, the one named last changes fastest.
Arguments:
- tokens: bfloat16 [512, 6144], P(('section', 'expert'), 'tensor'), may hold values from -6 to 6
- routes: int32 [512, 2], P(('section', 'expert')), may hold values from 0 to 7, all different within a row; in each aligned block of 8 rows (0 to 7, 8 to 15, ...) at most 4 rows name the same one
- router: float32 [6144, 8], replicated, may hold values from -0.18 to 0.18
- gate_proj: bfloat16 [8, 6144, 8192], P('expert', None, ('section', 'tensor')), may hold values from -0.078125 to 0.078125
- up_proj: bfloat16 [8, 6144, 8192], P('expert', None, ('section', 'tensor')), may hold values from -0.078125 to 0.078125
- down_proj: bfloat16 [8, 8192, 6144], P('expert', ('section', 'tensor')), may hold values from -0.125 to 0.125
- grad_out: bfloat16 [512, 6144], P(('section', 'expert'), 'tensor'), may hold values from -6 to 6
Outputs:
- moe_out: bfloat16 [512, 6144], P(('section', 'expert'), 'tensor')
- grad_tokens: bfloat16 [512, 6144], P(('section', 'expert'), 'tensor')
- grad_router: float32 [6144, 8], P('tensor')
Inputs may be any that keep to these rules, and one draw needn't show every extreme that they name: `routes`: each token names 2 different experts; in each aligned block of 8 tokens (the tokens of one group) no expert is named by more than 4 tokens, and in some blocks one expert is named by exactly 4.
All inputs are finite; a program needn't handle non-finite values.
Results may differ from a plain program's by a relative error of at most 0.02.
Values may be sent and summed in bfloat16 or wider, within the bound.
No kernel may reach another device: no remote copies, remote signals or barrier semaphores. Data moves between devices by JAX's collectives and lax.ppermute only.
A program may use at most 64 MiB of HBM per device.

v0:
```python
import jax
import jax.numpy as jnp
from jax import lax
from jax.sharding import PartitionSpec as P

precise = lax.Precision.HIGHEST


def route_table(routes, expert_count, capacity):
    flat_ids = routes.reshape(-1)
    expert_hot = (flat_ids[:, None] == jnp.arange(expert_count, dtype=jnp.int32)[None, :]).astype(
        jnp.float32
    )
    earlier = jnp.cumsum(expert_hot, axis=0) - expert_hot
    slot_ids = jnp.sum(earlier * expert_hot, axis=1).astype(jnp.int32)
    slot_hot = (slot_ids[:, None] == jnp.arange(capacity, dtype=jnp.int32)[None, :]).astype(
        jnp.float32
    )
    routing = expert_hot.T[:, None, :] * slot_hot.T[None, :, :]
    return routing.reshape(expert_count * capacity, flat_ids.shape[0])


def gate_weights(logits, routes):
    chosen = jnp.take_along_axis(logits, routes, axis=1)
    scores = jax.nn.sigmoid(chosen)
    totals = jnp.sum(scores, axis=1, keepdims=True)
    return (scores, scores / totals)


def expert_front(rows_x, gate_mat, up_mat):
    pre_gate = jnp.dot(rows_x, gate_mat, preferred_element_type=jnp.float32)
    pre_up = jnp.dot(rows_x, up_mat, preferred_element_type=jnp.float32)
    gate_sig = jax.nn.sigmoid(pre_gate)
    gate_act = pre_gate * gate_sig
    hidden = (gate_act * pre_up).astype(jnp.bfloat16)
    return (pre_gate, pre_up, gate_sig, gate_act, hidden)


def expert_grads(grad_hidden, pre_gate, pre_up, gate_sig, gate_act):
    grad_gate = (grad_hidden * pre_up * gate_sig * (1.0 + pre_gate * (1.0 - gate_sig))).astype(
        jnp.bfloat16
    )
    grad_up = (grad_hidden * gate_act).astype(jnp.bfloat16)
    return (grad_gate, grad_up)


def router_grads(grad_weight, scores, routes, expert_count):
    totals = scores[:, 0] + scores[:, 1]
    first = (grad_weight[:, 0] - grad_weight[:, 1]) * scores[:, 1] / (totals * totals)
    second = (grad_weight[:, 1] - grad_weight[:, 0]) * scores[:, 0] / (totals * totals)
    grad_scores = jnp.stack([first, second], axis=1)
    grad_chosen = grad_scores * scores * (1.0 - scores)
    expert_hot = (
        routes[:, :, None] == jnp.arange(expert_count, dtype=jnp.int32)[None, None, :]
    ).astype(jnp.float32)
    return jnp.sum(expert_hot * grad_chosen[:, :, None], axis=1)


def contract_last(left, right):
    return lax.dot_general(
        left, right, (((1,), (1,)), ((), ())), preferred_element_type=jnp.float32
    )


def on_device(tokens, routes, router, gate_proj, up_proj, down_proj, grad_out):
    tok_rows, quarter = tokens.shape
    tensor_count = lax.axis_size("tensor")
    expert_count = lax.axis_size("expert")
    top_count = routes.shape[1]
    capacity = 2 * tok_rows * top_count // expert_count
    block_rows = expert_count * capacity
    tensor_index = lax.axis_index("tensor")
    router_rows = lax.dynamic_slice_in_dim(router, tensor_index * quarter, quarter, 0)
    routing = route_table(routes, expert_count, capacity)
    gate_mat = gate_proj[0]
    up_mat = up_proj[0]
    down_mat = down_proj[0]
    send_x, send_dy = (tokens, grad_out)
    logits = lax.psum(jnp.dot(tokens.astype(jnp.float32), router_rows, precision=precise), "tensor")
    scores, weight = gate_weights(logits, routes)
    row_width = send_x.shape[1]
    x_sent = jnp.dot(
        routing, jnp.repeat(send_x.astype(jnp.float32), top_count, axis=0), precision=precise
    )
    x_sent = x_sent.astype(jnp.bfloat16).reshape(expert_count, capacity, row_width)
    scaled = jnp.repeat(send_dy.astype(jnp.float32), top_count, axis=0) * weight.reshape(-1, 1)
    dy_sent = (
        jnp.dot(routing, scaled, precision=precise)
        .astype(jnp.bfloat16)
        .reshape(expert_count, capacity, row_width)
    )

    def block_ids(count):
        return jnp.arange(count // block_rows, dtype=jnp.int32)

    def forward_block(hidden, block):
        section_at = block // tensor_count
        tensor_at = block % tensor_count
        hidden_rows = lax.dynamic_slice_in_dim(hidden, section_at * block_rows, block_rows, 0)
        columns = lax.dynamic_slice_in_dim(down_mat, tensor_at * quarter, quarter, 1)
        return jnp.dot(hidden_rows, columns, preferred_element_type=jnp.float32)

    def backward_block(grad_gate, grad_up, block):
        section_at = block // tensor_count
        tensor_at = block % tensor_count
        gate_rows = lax.dynamic_slice_in_dim(grad_gate, section_at * block_rows, block_rows, 0)
        up_rows = lax.dynamic_slice_in_dim(grad_up, section_at * block_rows, block_rows, 0)
        gate_part = lax.dynamic_slice_in_dim(gate_mat, tensor_at * quarter, quarter, 0)
        up_part = lax.dynamic_slice_in_dim(up_mat, tensor_at * quarter, quarter, 0)
        return contract_last(gate_rows, gate_part) + contract_last(up_rows, up_part)

    landed_x = lax.all_to_all(x_sent, "expert", split_axis=0, concat_axis=0, tiled=True)
    landed_x = lax.all_gather(landed_x, "tensor", axis=2, tiled=True)
    rows_x = lax.all_gather(landed_x.reshape(block_rows, -1), "section", axis=0, tiled=True)
    pre_gate, pre_up, gate_sig, gate_act, hidden = expert_front(rows_x, gate_mat, up_mat)
    summed_out = lax.psum_scatter(
        lax.map(
            lambda block: forward_block(hidden, block),
            block_ids(lax.axis_size(("section", "tensor")) * block_rows),
        )
        .reshape(lax.axis_size(("section", "tensor")) * block_rows, quarter)
        .astype(jnp.bfloat16),
        ("section", "tensor"),
        scatter_dimension=0,
        tiled=True,
    ).astype(jnp.float32)
    expert_out = lax.all_to_all(
        summed_out.reshape(expert_count, capacity, quarter).astype(jnp.bfloat16),
        "expert",
        split_axis=0,
        concat_axis=0,
        tiled=True,
    ).astype(jnp.float32)
    landed_dy = lax.all_to_all(dy_sent, "expert", split_axis=0, concat_axis=0, tiled=True)
    landed_dy = lax.all_gather(landed_dy, "tensor", axis=2, tiled=True)
    rows_dy = lax.all_gather(landed_dy.reshape(block_rows, -1), "section", axis=0, tiled=True)
    grad_hidden = contract_last(rows_dy, down_mat)
    grad_gate, grad_up = expert_grads(grad_hidden, pre_gate, pre_up, gate_sig, gate_act)
    summed_grad = lax.psum_scatter(
        lax.map(
            lambda block: backward_block(grad_gate, grad_up, block),
            block_ids(lax.axis_size(("section", "tensor")) * block_rows),
        )
        .reshape(lax.axis_size(("section", "tensor")) * block_rows, quarter)
        .astype(jnp.bfloat16),
        ("section", "tensor"),
        scatter_dimension=0,
        tiled=True,
    ).astype(jnp.float32)
    expert_grad = lax.all_to_all(
        summed_grad.reshape(expert_count, capacity, quarter).astype(jnp.bfloat16),
        "expert",
        split_axis=0,
        concat_axis=0,
        tiled=True,
    ).astype(jnp.float32)
    out_route = jnp.dot(
        routing.T, expert_out.reshape(block_rows, quarter), precision=precise
    ).reshape(tok_rows, top_count, quarter)
    grad_route = jnp.dot(
        routing.T, expert_grad.reshape(block_rows, quarter), precision=precise
    ).reshape(tok_rows, top_count, quarter)
    moe_out = jnp.sum(weight[:, :, None] * out_route, axis=1).astype(jnp.bfloat16)
    weight_part = jnp.sum(grad_out.astype(jnp.float32)[:, None, :] * out_route, axis=2)
    grad_weight = lax.psum(weight_part, "tensor")
    grad_logits = router_grads(grad_weight, scores, routes, expert_count)
    grad_tokens = (
        jnp.sum(grad_route, axis=1) + jnp.dot(grad_logits, router_rows.T, precision=precise)
    ).astype(jnp.bfloat16)
    router_part = jnp.dot(tokens.astype(jnp.float32).T, grad_logits, precision=precise)
    grad_router = lax.psum(router_part, ("section", "expert"))
    return (moe_out, grad_tokens, grad_router)


def solution(mesh):
    return jax.shard_map(
        on_device,
        mesh=mesh,
        in_specs=(
            P(("section", "expert"), "tensor"),
            P(("section", "expert"), None),
            P(),
            P("expert", None, ("section", "tensor")),
            P("expert", None, ("section", "tensor")),
            P("expert", ("section", "tensor"), None),
            P(("section", "expert"), "tensor"),
        ),
        out_specs=(
            P(("section", "expert"), "tensor"),
            P(("section", "expert"), "tensor"),
            P("tensor", None),
        ),
        check_vma=False,
    )
```

profile of v0, /device:TPU:8, one launch (start us, length us, event | category | flops | bytes accessed | tf_op | source)
XLA Modules:
  0.0 1154.4 jit_solution(11186698686855565210)
XLA Ops:
  9.6 12.0 %all_to_all.20 = bf16[8,4,1536]{2,1,0:T(4,128)(2,1)S(1)} all-to-all(bf16[8,4,1536]{2,1,0:T(4,128)(2,1)S(1)} %reshape.192), channel_id=1, replica_groups=mesh['section'=8,'expert'=8,'tensor'=4] {'expert'}, dimensions={0} | all-to-all | bytes 196608 | tf_op jit(solution)/shard_map/all_to_all | solution.py:112
  21.7 13.1 %all_gather.12 = bf16[8,4,6144]{2,1,0:T(4,128)(2,1)S(1)} all-gather(bf16[8,4,1536]{2,1,0:T(4,128)(2,1)S(1)} %all_to_all.20), channel_id=1, replica_groups=mesh['section'=8,'expert'=8,'tensor'=4] {'tensor'}, dimensions={2}, use_global_device_ids=true | all-gather | bytes 491520 | tf_op jit(solution)/shard_map/all_gather | solution.py:113
  37.5 8.1 psum.21
  47.0 16.7 %all_to_all.21 = bf16[8,4,1536]{2,1,0:T(4,128)(2,1)S(1)} all-to-all(bf16[8,4,1536]{2,1,0:T(4,128)(2,1)S(1)} %reshape.195), channel_id=1, replica_groups=mesh['section'=8,'expert'=8,'tensor'=4] {'expert'}, dimensions={0} | all-to-all | bytes 196608 | tf_op jit(solution)/shard_map/all_to_all | solution.py:134
  63.7 12.4 %all_gather.14 = bf16[8,4,6144]{2,1,0:T(4,128)(2,1)S(1)} all-gather(bf16[8,4,1536]{2,1,0:T(4,128)(2,1)S(1)} %all_to_all.21), channel_id=1, replica_groups=mesh['section'=8,'expert'=8,'tensor'=4] {'tensor'}, dimensions={2}, use_global_device_ids=true | all-gather | bytes 491520 | tf_op jit(solution)/shard_map/all_gather | solution.py:135
  77.1 51.9 %all-gather.3.cloned.1.call-done = bf16[256,6144]{1,0:T(8,128)(2,1)} async-done(((bf16[32,6144]{1,0:T(8,128)(2,1)}), bf16[256,6144]{1,0:T(8,128)(2,1)}) %all-gather.3.cloned.1.call-update) | async-done | bytes 3145744 | tf_op jit(solution)/shard_map/all_gather | solution.py:114
  129.0 4.7 fusion.29
  133.7 1.7 fusion.31
  135.4 83.3 %all-gather.5.cloned.1.call-done = bf16[256,6144]{1,0:T(8,128)(2,1)} async-done(((bf16[32,6144]{1,0:T(8,128)(2,1)}), bf16[256,6144]{1,0:T(8,128)(2,1)}) %all-gather.5.cloned.1.call-update) | async-done | bytes 3145744 | tf_op jit(solution)/shard_map/all_gather | solution.py:136
  218.7 4.6 multiply_convert_fusion
  223.7 147.5 %while.24 = (s32[]{:T(128)}, bf16[32,32,1536]{2,1,0:T(8,128)(2,1)S(1)}, s32[32]{0:T(128)S(1)}, bf16[256,256]{1,0:T(8,128)(2,1)}, bf16[256,6144]{1,0:T(8,128)(2,1...) while((s32[]{:T(128)}, ...), condition=%wide.region_5.6_spmd, body=%wide.region_4.5_spmd.sunk | while | flops 25165852 | bytes 999876 | solution.py:117
  371.1 1.7 copy-done.2
  373.2 198.6 %while.25 = (s32[]{:T(128)}, bf16[32,32,1536]{2,1,0:T(8,128)(2,1)S(1)}, s32[32]{0:T(128)S(1)}, bf16[256,256]{1,0:T(8,128)(2,1)}, bf16[6144,256]{1,0:T(8,128)(2,1...) while((s32[]{:T(128)}, ...), condition=%wide.region_9.10_spmd, body=%wide.region_8.9_spmd.sunk | while | flops 50380828 | bytes 2195932 | solution.py:140
  377.9 1.5 fusion.64
  384.1 1.5 fusion.64
  388.9 1.5 fusion.63
  390.4 1.5 fusion.64
  395.1 1.5 fusion.63
  396.6 1.5 fusion.64
  402.8 1.5 fusion.64
  407.5 1.5 fusion.63
  409.0 1.5 fusion.64
  415.2 1.5 fusion.64
  419.9 1.5 fusion.63
  421.4 1.5 fusion.64
  427.6 1.5 fusion.64
  432.3 1.5 fusion.63
  433.8 1.5 fusion.64
  440.0 1.5 fusion.64
  446.2 1.5 fusion.64
  452.5 1.5 fusion.64
  457.2 1.5 fusion.63
  458.7 1.5 fusion.64
  464.9 1.5 fusion.64
  471.1 1.5 fusion.64
  477.3 1.5 fusion.64
  483.5 1.5 fusion.64
  489.7 1.5 fusion.64
  494.4 1.5 fusion.63
  495.9 1.5 fusion.64
  500.6 1.5 fusion.63
  502.1 1.5 fusion.64
  508.3 1.5 fusion.64
  514.5 1.5 fusion.64
  520.7 1.5 fusion.64
  526.9 1.5 fusion.64
  533.1 1.5 fusion.64
  539.3 1.5 fusion.64
  545.5 1.5 fusion.64
  550.3 1.5 fusion.63
  551.8 1.5 fusion.64
  558.0 1.5 fusion.64
  562.7 1.5 fusion.63
  564.2 1.5 fusion.64
  570.4 1.5 fusion.64
  571.9 1.7 copy-done.1
  573.6 52.4 %reduce-scatter.3.cloned.1.call-done = bf16[32,1536]{1,0:T(8,128)(2,1)} async-done(((bf16[1024,1536]{1,0:T(8,128)(2,1)}), bf16[32,1536]{1,0:T(8,128)(2,1)}) %reduce-scatter.3.cloned.1.call-update) | async-done | bytes 98320 | tf_op jit(solution)/shard_map/reduce_scatter | solution.py:116
  626.0 1.5 convert_element_type.89
  627.5 3.4 all-to-all-start.1
  631.0 253.9 %reduce-scatter.5.cloned.1.call-done = bf16[32,1536]{1,0:T(8,128)(2,1)} async-done(((bf16[1024,1536]{1,0:T(8,128)(2,1)}), bf16[32,1536]{1,0:T(8,128)(2,1)}) %reduce-scatter.5.cloned.1.call-update) | async-done | bytes 98320 | tf_op jit(solution)/shard_map/reduce_scatter | solution.py:139
  884.9 1.6 convert_element_type.97
  886.4 3.4 all-to-all-start.3
  890.6 9.5 psum.22
  900.4 246.4 %psum.23 = f32[1536,8]{0,1:T(8,128)} all-reduce(f32[1536,8]{0,1:T(8,128)S(1)} %convolution_bitcast_fusion.1), channel_id=1, replica_groups=mesh['section'=8,'expert'=8,'tensor'=4] {'section','expert'}, use_global_device_ids=true, to_apply=%region_15.16 | all-reduce | flops 12288 | bytes 98304 | tf_op jit(solution)/shard_map/psum | solution.py:171
  (186 shorter events, 125.3 us)
Async XLA Ops:
  7.2 29.4 %copy-start = (f32[6144,8]{0,1:T(8,128)S(1)}, f32[6144,8]{0,1:T(8,128)}, u32[]{:S(2)}) copy-start(f32[6144,8]{0,1:T(8,128)} %param.13) | copy-start | bytes 589828
  7.2 121.8 %all-gather.3.cloned.1.call-start = ((), (), s32[]{:S(2)}) async-start(), calls=%async_computation.6 | async-start | bytes 3538944 | tf_op jit(solution)/shard_map/all_gather | solution.py:114
  9.6 36.7 %copy-start.5 = (bf16[8,1536]{1,0:T(8,128)(2,1)S(1)}, bf16[8,1536]{1,0:T(8,128)(2,1)}, u32[]{:S(2)}) copy-start(bf16[8,1536]{1,0:T(8,128)(2,1)} %param.17) | copy-start | bytes 73732
  9.6 36.7 %copy-start.6 = (s32[8,2]{0,1:T(2,128)S(1)}, s32[8,2]{0,1:T(2,128)}, u32[]{:S(2)}) copy-start(s32[8,2]{0,1:T(2,128)} %param.12) | copy-start | bytes 196
  35.7 183.0 %all-gather.5.cloned.1.call-start = ((), (), s32[]{:S(2)}) async-start(), calls=%async_computation.8 | async-start | bytes 3538944 | tf_op jit(solution)/shard_map/all_gather | solution.py:136
  77.0 549.0 %reduce-scatter.3.cloned.1.call-start = ((), (), s32[]{:S(2)}) async-start(), calls=%async_computation.7 | async-start | bytes 3244032 | tf_op jit(solution)/shard_map/reduce_scatter | solution.py:116
  77.0 56.6 %copy-start.3 = (bf16[1,6144,256]{2,1,0:T(8,128)(2,1)S(1)}, bf16[1,6144,256]{2,1,0:T(8,128)(2,1)}, u32[]{:S(2)}) copy-start(bf16[1,6144,256]{2,1,0:T(8,128)(2,1)} %param.14) | copy-start | bytes 9437188
  129.0 4.7 copy-start.7
  371.1 1.7 copy-start.2
  372.8 512.0 %reduce-scatter.5.cloned.1.call-start = ((), (), s32[]{:S(2)}) async-start(), calls=%async_computation.9 | async-start | bytes 3244032 | tf_op jit(solution)/shard_map/reduce_scatter | solution.py:139
  571.9 1.7 copy-start.1
  571.9 328.3 %copy-start.4 = (bf16[8,1536]{1,0:T(8,128)(2,1)S(1)}, bf16[8,1536]{1,0:T(8,128)(2,1)}, u32[]{:S(2)}) copy-start(bf16[8,1536]{1,0:T(8,128)(2,1)} %param.11) | copy-start | bytes 73732
  627.5 258.9 %all-to-all-start.1 = ((bf16[8,4,1536]{2,1,0:T(4,128)(2,1)}), bf16[8,4,1536]{2,1,0:T(4,128)(2,1)S(1)}, u32[]{:S(2)}, u32[]{:S(2)}) async-start(bf16[8,4,1536]{2,1,0:T(4,128)(2,1)} %convert_element_type.89), calls=%async_computation.2 | async-start | bytes 196608 | tf_op jit(solution)/shard_map/all_to_all | solution.py:127
  886.4 260.4 %all-to-all-start.3 = ((bf16[8,4,1536]{2,1,0:T(4,128)(2,1)}), bf16[8,4,1536]{2,1,0:T(4,128)(2,1)S(1)}, u32[]{:S(2)}, u32[]{:S(2)}) async-start(bf16[8,4,1536]{2,1,0:T(4,128)(2,1)} %convert_element_type.97), calls=%async_computation.5 | async-start | bytes 196608 | tf_op jit(solution)/shard_map/all_to_all | solution.py:150
Sparse Core Ops, SparseCore 0:
  35.8 93.1 all-gather.2
  131.6 87.0 all-gather.4
  373.0 252.9 reduce-scatter.2
  632.1 252.7 reduce-scatter.4
where the time goes:
time: 1160 us; the launch traced here: 1150 us
  waiting for transfers between devices  442 us (38%)
  blocking collectives  318 us (27%)
  loops' own time  169 us (15%)
  matrix products  154 us (13%)
  local copies, waits for them, and re-layouts  50 us (4%)
  between operations  14 us (1%)
    reduce_scatter x1, waiting for transfers between devices, on_device(): lax.psum_scatter(lax.map(lambda block: backward_block(grad_gate, grad_up,...  254 us
    psum x1, blocking collectives, on_device(): grad_router = lax.psum(router_part, ('section', 'expert'))  246 us
    dot_general x65, matrix products, contract_last(): lax.dot_general(left, right, (((1,), (1,)), ((), ())), preferred_element_...  99.8 us
    another operation x1, loops' own time, on_device(): lax.map(lambda block: backward_block(grad_gate, grad_up, block), block_id...  84.7 us
    another operation x1, loops' own time, on_device(): lax.map(lambda block: forward_block(hidden, block), block_ids(lax.axis_si...  83.9 us
    all_gather x1, waiting for transfers between devices, on_device(): lax.all_gather(landed_dy.reshape(block_rows, -1), 'section', axis=0, tile...  83.3 us
    reduce_scatter x1, waiting for transfers between devices, on_device(): lax.psum_scatter(lax.map(lambda block: forward_block(hidden, block), bloc...  52.4 us
    all_gather x1, waiting for transfers between devices, on_device(): lax.all_gather(landed_x.reshape(block_rows, -1), 'section', axis=0, tiled...  51.9 us
  transfers between devices with their start and end apart: 6, of which 4 were waited for; matrix products, arithmetic and copies ran while one was open for 11% of the time, Pallas kernels for 0%

commit v1 on v0

--- a/solution.py
+++ b/solution.py
@@ -168,7 +168,7 @@
         jnp.sum(grad_route, axis=1) + jnp.dot(grad_logits, router_rows.T, precision=precise)
     ).astype(jnp.bfloat16)
     router_part = jnp.dot(tokens.astype(jnp.float32).T, grad_logits, precision=precise)
-    grad_router = lax.psum(router_part, ("section", "expert"))
+    grad_router = lax.psum(lax.psum(router_part, "expert"), "section")
     return (moe_out, grad_tokens, grad_router)
 
 

time: 1160 us -> 994 us (0.86)
  blocking collectives: 318 us -> 149 us
    psum x1 -> x2, blocking collectives: 246 us -> 77.4 us  [on_device(): grad_router = lax.psum(lax.psum(router_part, 'expert'), 'section')]
  transfers between devices with their start and end apart: 6 -> 6, of which waited for: 4 -> 4; matrix products, arithmetic and copies ran while one was open for 11% -> 13% of each run, Pallas kernels for 0% -> 0%
where the time goes in v1:
time: 994 us; the launch traced here: 985 us
  waiting for transfers between devices  442 us (44%)
  loops' own time  169 us (17%)
  matrix products  154 us (15%)
  blocking collectives  149 us (15%)
  local copies, waits for them, and re-layouts  50 us (5%)
  between operations  14 us (1%)
    reduce_scatter x1, waiting for transfers between devices, on_device(): lax.psum_scatter(lax.map(lambda block: backward_block(grad_gate, grad_up,...  254 us
    dot_general x65, matrix products, contract_last(): lax.dot_general(left, right, (((1,), (1,)), ((), ())), preferred_element_...  99.8 us
    another operation x1, loops' own time, on_device(): lax.map(lambda block: backward_block(grad_gate, grad_up, block), block_id...  84.7 us
    another operation x1, loops' own time, on_device(): lax.map(lambda block: forward_block(hidden, block), block_ids(lax.axis_si...  83.9 us
    all_gather x1, waiting for transfers between devices, on_device(): lax.all_gather(landed_dy.reshape(block_rows, -1), 'section', axis=0, tile...  83.3 us
    psum x2, blocking collectives, on_device(): grad_router = lax.psum(lax.psum(router_part, 'expert'), 'section')  77.4 us
    reduce_scatter x1, waiting for transfers between devices, on_device(): lax.psum_scatter(lax.map(lambda block: forward_block(hidden, block), bloc...  52.4 us
    all_gather x1, waiting for transfers between devices, on_device(): lax.all_gather(landed_x.reshape(block_rows, -1), 'section', axis=0, tiled...  51.9 us
  transfers between devices with their start and end apart: 6, of which 4 were waited for; matrix products, arithmetic and copies ran while one was open for 13% of the time, Pallas kernels for 0%

profile of v1, /device:TPU:8, one launch (start us, length us, event | category | flops | bytes accessed | tf_op | source)
XLA Modules:
  0.0 985.4 jit_solution(15117982494095900104)
XLA Ops:
  9.6 12.0 %all_to_all.20 = bf16[8,4,1536]{2,1,0:T(4,128)(2,1)S(1)} all-to-all(bf16[8,4,1536]{2,1,0:T(4,128)(2,1)S(1)} %reshape.192), channel_id=1, replica_groups=mesh['section'=8,'expert'=8,'tensor'=4] {'expert'}, dimensions={0} | all-to-all | bytes 196608 | tf_op jit(solution)/shard_map/all_to_all | solution.py:112
  21.7 13.1 %all_gather.12 = bf16[8,4,6144]{2,1,0:T(4,128)(2,1)S(1)} all-gather(bf16[8,4,1536]{2,1,0:T(4,128)(2,1)S(1)} %all_to_all.20), channel_id=1, replica_groups=mesh['section'=8,'expert'=8,'tensor'=4] {'tensor'}, dimensions={2}, use_global_device_ids=true | all-gather | bytes 491520 | tf_op jit(solution)/shard_map/all_gather | solution.py:113
  37.5 8.1 psum.28
  47.0 16.7 %all_to_all.21 = bf16[8,4,1536]{2,1,0:T(4,128)(2,1)S(1)} all-to-all(bf16[8,4,1536]{2,1,0:T(4,128)(2,1)S(1)} %reshape.195), channel_id=1, replica_groups=mesh['section'=8,'expert'=8,'tensor'=4] {'expert'}, dimensions={0} | all-to-all | bytes 196608 | tf_op jit(solution)/shard_map/all_to_all | solution.py:134
  63.7 12.4 %all_gather.14 = bf16[8,4,6144]{2,1,0:T(4,128)(2,1)S(1)} all-gather(bf16[8,4,1536]{2,1,0:T(4,128)(2,1)S(1)} %all_to_all.21), channel_id=1, replica_groups=mesh['section'=8,'expert'=8,'tensor'=4] {'tensor'}, dimensions={2}, use_global_device_ids=true | all-gather | bytes 491520 | tf_op jit(solution)/shard_map/all_gather | solution.py:135
  77.1 51.9 %all-gather.3.cloned.1.call-done = bf16[256,6144]{1,0:T(8,128)(2,1)} async-done(((bf16[32,6144]{1,0:T(8,128)(2,1)}), bf16[256,6144]{1,0:T(8,128)(2,1)}) %all-gather.3.cloned.1.call-update) | async-done | bytes 3145744 | tf_op jit(solution)/shard_map/all_gather | solution.py:114
  129.0 4.7 fusion.29
  133.7 1.7 fusion.31
  135.4 83.3 %all-gather.5.cloned.1.call-done = bf16[256,6144]{1,0:T(8,128)(2,1)} async-done(((bf16[32,6144]{1,0:T(8,128)(2,1)}), bf16[256,6144]{1,0:T(8,128)(2,1)}) %all-gather.5.cloned.1.call-update) | async-done | bytes 3145744 | tf_op jit(solution)/shard_map/all_gather | solution.py:136
  218.7 4.6 multiply_convert_fusion
  223.7 147.5 %while.24 = (s32[]{:T(128)}, bf16[32,32,1536]{2,1,0:T(8,128)(2,1)S(1)}, s32[32]{0:T(128)S(1)}, bf16[256,256]{1,0:T(8,128)(2,1)}, bf16[256,6144]{1,0:T(8,128)(2,1...) while((s32[]{:T(128)}, ...), condition=%wide.region_5.6_spmd, body=%wide.region_4.5_spmd.sunk | while | flops 25165852 | bytes 999876 | solution.py:117
  371.1 1.7 copy-done.2
  373.2 198.6 %while.25 = (s32[]{:T(128)}, bf16[32,32,1536]{2,1,0:T(8,128)(2,1)S(1)}, s32[32]{0:T(128)S(1)}, bf16[256,256]{1,0:T(8,128)(2,1)}, bf16[6144,256]{1,0:T(8,128)(2,1...) while((s32[]{:T(128)}, ...), condition=%wide.region_9.10_spmd, body=%wide.region_8.9_spmd.sunk | while | flops 50380828 | bytes 2195932 | solution.py:140
  377.9 1.5 fusion.64
  384.1 1.5 fusion.64
  390.4 1.5 fusion.64
  395.1 1.5 fusion.63
  396.6 1.5 fusion.64
  402.8 1.5 fusion.64
  407.5 1.5 fusion.63
  409.0 1.5 fusion.64
  415.2 1.5 fusion.64
  419.9 1.5 fusion.63
  421.4 1.5 fusion.64
  427.6 1.5 fusion.64
  432.3 1.5 fusion.63
  433.8 1.5 fusion.64
  440.0 1.5 fusion.64
  446.2 1.5 fusion.64
  452.5 1.5 fusion.64
  457.2 1.5 fusion.63
  458.7 1.5 fusion.64
  464.9 1.5 fusion.64
  471.1 1.5 fusion.64
  477.3 1.5 fusion.64
  483.5 1.5 fusion.64
  489.7 1.5 fusion.64
  494.4 1.5 fusion.63
  495.9 1.5 fusion.64
  500.6 1.5 fusion.63
  502.1 1.5 fusion.64
  508.3 1.5 fusion.64
  514.5 1.5 fusion.64
  520.7 1.5 fusion.64
  526.9 1.5 fusion.64
  533.1 1.5 fusion.64
  539.3 1.5 fusion.64
  545.5 1.5 fusion.64
  550.3 1.5 fusion.63
  551.8 1.5 fusion.64
  558.0 1.5 fusion.64
  562.7 1.5 fusion.63
  564.2 1.5 fusion.64
  570.4 1.5 fusion.64
  571.9 1.7 copy-done.1
  573.6 52.4 %reduce-scatter.3.cloned.1.call-done = bf16[32,1536]{1,0:T(8,128)(2,1)} async-done(((bf16[1024,1536]{1,0:T(8,128)(2,1)}), bf16[32,1536]{1,0:T(8,128)(2,1)}) %reduce-scatter.3.cloned.1.call-update) | async-done | bytes 98320 | tf_op jit(solution)/shard_map/reduce_scatter | solution.py:116
  626.0 1.5 convert_element_type.89
  627.5 3.4 all-to-all-start.1
  631.0 253.9 %reduce-scatter.5.cloned.1.call-done = bf16[32,1536]{1,0:T(8,128)(2,1)} async-done(((bf16[1024,1536]{1,0:T(8,128)(2,1)}), bf16[32,1536]{1,0:T(8,128)(2,1)}) %reduce-scatter.5.cloned.1.call-update) | async-done | bytes 98320 | tf_op jit(solution)/shard_map/reduce_scatter | solution.py:139
  884.9 1.6 convert_element_type.97
  886.4 3.4 all-to-all-start.3
  890.6 9.5 psum.29
  900.4 27.7 %psum.30 = f32[1536,8]{0,1:T(8,128)S(1)} all-reduce(f32[1536,8]{0,1:T(8,128)S(1)} %convolution_bitcast_fusion.1), channel_id=1, replica_groups=mesh['section'=8,'expert'=8,'tensor'=4] {'expert'}, use_global_device_ids=true, to_apply=%region_15.16 | all-reduce | flops 12288 | bytes 98304 | tf_op jit(solution)/shard_map/psum | solution.py:171
  928.1 49.7 %psum.31 = f32[1536,8]{0,1:T(8,128)} all-reduce(f32[1536,8]{0,1:T(8,128)S(1)} %psum.30), channel_id=1, replica_groups=mesh['section'=8,'expert'=8,'tensor'=4] {'section'}, use_global_device_ids=true, to_apply=%region_16.17 | all-reduce | flops 12288 | bytes 98304 | tf_op jit(solution)/shard_map/psum | solution.py:171
  (187 shorter events, 126.8 us)
Async XLA Ops:
  7.2 29.4 %copy-start = (f32[6144,8]{0,1:T(8,128)S(1)}, f32[6144,8]{0,1:T(8,128)}, u32[]{:S(2)}) copy-start(f32[6144,8]{0,1:T(8,128)} %param.13) | copy-start | bytes 589828
  7.2 121.8 %all-gather.3.cloned.1.call-start = ((), (), s32[]{:S(2)}) async-start(), calls=%async_computation.6 | async-start | bytes 3538944 | tf_op jit(solution)/shard_map/all_gather | solution.py:114
  9.6 36.7 %copy-start.5 = (bf16[8,1536]{1,0:T(8,128)(2,1)S(1)}, bf16[8,1536]{1,0:T(8,128)(2,1)}, u32[]{:S(2)}) copy-start(bf16[8,1536]{1,0:T(8,128)(2,1)} %param.17) | copy-start | bytes 73732
  9.6 36.7 %copy-start.6 = (s32[8,2]{0,1:T(2,128)S(1)}, s32[8,2]{0,1:T(2,128)}, u32[]{:S(2)}) copy-start(s32[8,2]{0,1:T(2,128)} %param.12) | copy-start | bytes 196
  35.7 183.0 %all-gather.5.cloned.1.call-start = ((), (), s32[]{:S(2)}) async-start(), calls=%async_computation.8 | async-start | bytes 3538944 | tf_op jit(solution)/shard_map/all_gather | solution.py:136
  77.0 549.0 %reduce-scatter.3.cloned.1.call-start = ((), (), s32[]{:S(2)}) async-start(), calls=%async_computation.7 | async-start | bytes 3244032 | tf_op jit(solution)/shard_map/reduce_scatter | solution.py:116
  77.0 56.6 %copy-start.3 = (bf16[1,6144,256]{2,1,0:T(8,128)(2,1)S(1)}, bf16[1,6144,256]{2,1,0:T(8,128)(2,1)}, u32[]{:S(2)}) copy-start(bf16[1,6144,256]{2,1,0:T(8,128)(2,1)} %param.14) | copy-start | bytes 9437188
  129.0 4.7 copy-start.7
  371.1 1.7 copy-start.2
  372.8 512.0 %reduce-scatter.5.cloned.1.call-start = ((), (), s32[]{:S(2)}) async-start(), calls=%async_computation.9 | async-start | bytes 3244032 | tf_op jit(solution)/shard_map/reduce_scatter | solution.py:139
  571.9 1.7 copy-start.1
  571.9 328.3 %copy-start.4 = (bf16[8,1536]{1,0:T(8,128)(2,1)S(1)}, bf16[8,1536]{1,0:T(8,128)(2,1)}, u32[]{:S(2)}) copy-start(bf16[8,1536]{1,0:T(8,128)(2,1)} %param.11) | copy-start | bytes 73732
  627.5 258.9 %all-to-all-start.1 = ((bf16[8,4,1536]{2,1,0:T(4,128)(2,1)}), bf16[8,4,1536]{2,1,0:T(4,128)(2,1)S(1)}, u32[]{:S(2)}, u32[]{:S(2)}) async-start(bf16[8,4,1536]{2,1,0:T(4,128)(2,1)} %convert_element_type.89), calls=%async_computation.2 | async-start | bytes 196608 | tf_op jit(solution)/shard_map/all_to_all | solution.py:127
  886.4 91.4 %all-to-all-start.3 = ((bf16[8,4,1536]{2,1,0:T(4,128)(2,1)}), bf16[8,4,1536]{2,1,0:T(4,128)(2,1)S(1)}, u32[]{:S(2)}, u32[]{:S(2)}) async-start(bf16[8,4,1536]{2,1,0:T(4,128)(2,1)} %convert_element_type.97), calls=%async_computation.5 | async-start | bytes 196608 | tf_op jit(solution)/shard_map/all_to_all | solution.py:150
Sparse Core Ops, SparseCore 0:
  35.8 93.1 all-gather.2
  131.6 87.0 all-gather.4
  373.0 252.9 reduce-scatter.2
  632.1 252.7 reduce-scatter.4
